TPU v7x, 256 devices: a whole 4x4x8 slice. The times are simulated.
256 devices in a mesh: dp: 4 (over y), expert: 64 (over z, x, core).
Axes of the slice: x: 4, y: 4, z: 8, core: 2. Of those that a mesh axis runs over, the one named last changes fastest.
Arguments:
- tokens: bfloat16 [32768, 2048], P(('dp', 'expert')), may hold values from -6 to 6
- cotangent: bfloat16 [32768, 2048], P(('dp', 'expert')), may hold values from -3 to 3
- routes: int32 [32768, 1], P(('dp', 'expert')), may hold values from 0 to 63, as said below
- gate_fixed: int32 [32768, 1], P(('dp', 'expert')), may hold values from 8192 to 65535
- w_gate: bfloat16 [64, 2048, 768], P('expert', 'dp'), may hold values from -0.125 to 0.125
- w_up: bfloat16 [64, 2048, 768], P('expert', 'dp'), may hold values from -0.125 to 0.125
- w_down: bfloat16 [64, 768, 2048], P('expert', None, 'dp'), may hold values from -0.21875 to 0.21875
Outputs:
- mixed: bfloat16 [32768, 2048], P(('dp', 'expert'))
- grad_tokens: bfloat16 [32768, 2048], P(('dp', 'expert'))
- grad_w_gate: bfloat16 [64, 2048, 768], P('expert', 'dp')
- grad_w_up: bfloat16 [64, 2048, 768], P('expert', 'dp')
- grad_w_down: bfloat16 [64, 768, 2048], P('expert', None, 'dp')
Inputs may be any that keep to these rules, and one draw needn't show every extreme that they name: `routes`: each token names one expert. Among the tokens of one device no expert is named more than 3 times, and some experts are named exactly 3 times by the tokens of every device.
All inputs are finite; a program needn't handle non-finite values.
Results may differ from a plain program's by a relative error of at most 0.0058.
Values may be sent and summed in bfloat16 or wider, within the bound.
A program may use at most 64 MiB of HBM per device.

v0:
```python
import jax
import jax.numpy as jnp
from jax import lax
from jax.sharding import Mesh
from jax.sharding import PartitionSpec as P

EXPERT = ("expert_0", "expert_1", "expert_2")
DP_EXPERT = ("dp", "expert_0", "expert_1", "expert_2")


def in_blocks(array, dim, size):
    lengths = array.shape
    tiles = array.reshape(*lengths[:dim], size, lengths[dim] // size, *lengths[dim + 1 :])
    return jnp.moveaxis(tiles, dim, 0)


def joined_along(tiles, dim):
    tiles = jnp.moveaxis(tiles, 0, dim)
    lengths = tiles.shape
    return tiles.reshape(*lengths[:dim], lengths[dim] * lengths[dim + 1], *lengths[dim + 2 :])


def turned_blocks(tiles, axes, turns):
    lengths = [lax.axis_size(a) for a in axes]
    tiles = tiles.reshape(*lengths, *tiles.shape[1:])
    for k in turns:
        tiles = lax.all_to_all(tiles, axes[k], split_axis=k, concat_axis=k, tiled=True)
    return tiles.reshape(-1, *tiles.shape[len(axes) :])


def two_step_exchange(array, groups, turns, split_dim, concat_dim):
    size = lax.axis_size(groups[0]) * lax.axis_size(groups[1])
    tiles = in_blocks(array, split_dim, size)
    return joined_along(turned_blocks(tiles, groups, turns), concat_dim)


def gather_turned(arrays, axis, dims):
    turned = [jnp.moveaxis(a, dim, 0) for a, dim in zip(arrays, dims)]
    widths = [t[0].size for t in turned]
    both = jnp.concatenate([t.reshape(-1, w) for t, w in zip(turned, widths)], axis=1)
    filled = lax.all_gather(both, axis, axis=0, tiled=True)
    tiles = jnp.split(filled, [sum(widths[:k]) for k in range(1, len(widths))], axis=1)
    return tuple(
        (
            jnp.moveaxis(b.reshape(-1, *t.shape[1:]), 0, dim)
            for b, t, dim in zip(tiles, turned, dims)
        )
    )


def sent_together(arrays, axis, split_dim, concat_dim, along):
    ends, at = ([], 0)
    for a in arrays[:-1]:
        at += a.shape[along]
        ends.append(at)
    both = jnp.concatenate(arrays, axis=along)
    return tuple(
        jnp.split(
            lax.all_to_all(both, axis, split_axis=split_dim, concat_axis=concat_dim, tiled=True),
            ends,
            axis=along,
        )
    )


def in_one_piece(arrays, axis, dim, along):
    both = jnp.concatenate(arrays, axis=along)
    filled, at, gathered = (lax.all_gather(both, axis, axis=dim, tiled=True), 0, [])
    for a in arrays:
        gathered.append(lax.slice_in_dim(filled, at, at + a.shape[along], axis=along))
        at += a.shape[along]
    return tuple(gathered)


def swap_experts(buffer):
    return two_step_exchange(buffer, (("expert_0", "expert_1"), "expert_2"), (0, 1), 1, 1)


def contract_last(left_side, right_side):
    return lax.dot_general(
        left_side, right_side, (((1,), (1,)), ((), ())), preferred_element_type=jnp.float32
    )


def contract_first(left_side, right_side):
    return lax.dot_general(
        left_side, right_side, (((0,), (0,)), ((), ())), preferred_element_type=jnp.float32
    )


def gate_gradients(grad_hidden, gate_pre, up_pre):
    sigmoid_gate = jax.nn.sigmoid(gate_pre)
    grad_gate = grad_hidden * up_pre * sigmoid_gate * (1.0 + gate_pre * (1.0 - sigmoid_gate))
    grad_up = grad_hidden * gate_pre * sigmoid_gate
    return jnp.concatenate([grad_gate, grad_up], axis=1).astype(jnp.bfloat16)


def full_width_pass(outgoing, grad_outgoing, gate_up_w, down_all, shape_out):
    expert_count, capacity, model_width = shape_out
    own_rows = expert_count * capacity
    hidden_width = down_all.shape[0]
    received = swap_experts(outgoing)
    flat_received = received.reshape(own_rows, model_width)
    gate_up = jnp.dot(flat_received, gate_up_w, preferred_element_type=jnp.float32)
    gate_pre = gate_up[:, :hidden_width]
    up_pre = gate_up[:, hidden_width:]
    hidden = (gate_pre * jax.nn.sigmoid(gate_pre) * up_pre).astype(jnp.bfloat16)
    slot_out = jnp.dot(hidden, down_all, preferred_element_type=jnp.float32).astype(jnp.bfloat16)
    returned = swap_experts(slot_out.reshape(1, expert_count, capacity, model_width)).reshape(
        own_rows, model_width
    )
    grad_received = swap_experts(grad_outgoing)
    grad_hidden = contract_last(grad_received.reshape(own_rows, model_width), down_all)
    grad_gate_up = gate_gradients(grad_hidden, gate_pre, up_pre)
    slot_grad_in = contract_last(grad_gate_up, gate_up_w).astype(jnp.bfloat16)
    grad_returned = swap_experts(
        slot_grad_in.reshape(1, expert_count, capacity, model_width)
    ).reshape(own_rows, model_width)
    return (received, grad_received, hidden, grad_gate_up, returned, grad_returned)


def body(tokens, cotangent, routes, gate_fixed, w_gate, w_up, w_down):
    tok_count = tokens.shape[0]
    model_width = tokens.shape[1]
    route_count = routes.shape[1]
    hidden_width = w_gate.shape[2]
    expert_count = lax.axis_size(EXPERT)
    capacity = 3 * tok_count * route_count // (2 * expert_count)
    own_rows = expert_count * capacity
    flat_total = tok_count * route_count
    route_weight = gate_fixed.astype(jnp.float32) / 65536.0
    flat_routes = routes.reshape(flat_total)
    one_hot = (flat_routes[:, None] == jnp.arange(expert_count, dtype=jnp.int32)[None, :]).astype(
        jnp.int32
    )
    position = jnp.sum((jnp.cumsum(one_hot, axis=0) - one_hot) * one_hot, axis=1)
    slot_index = flat_routes * capacity + position
    matches = slot_index[None, :] == jnp.arange(own_rows, dtype=jnp.int32)[:, None]
    occupied = jnp.any(matches, axis=1)
    source_row = jnp.sum(
        jnp.where(matches, jnp.arange(flat_total, dtype=jnp.int32)[None, :], 0), axis=1
    )
    slot_weight = jnp.sum(
        jnp.where(matches, route_weight.reshape(flat_total)[None, :], 0.0), axis=1
    )
    token_row = source_row // route_count
    outgoing = jnp.where(
        occupied[:, None], jnp.take(tokens, token_row, axis=0), jnp.zeros((), tokens.dtype)
    )
    outgoing = outgoing.reshape(1, expert_count, capacity, model_width)
    scaled = (
        slot_weight[:, None] * jnp.take(cotangent, token_row, axis=0).astype(jnp.float32)
    ).astype(jnp.bfloat16)
    grad_outgoing = jnp.where(occupied[:, None], scaled, jnp.zeros((), scaled.dtype))
    grad_outgoing = grad_outgoing.reshape(1, expert_count, capacity, model_width)
    shape_out = (expert_count, capacity, model_width)
    replicas = lax.axis_size("dp")
    part_width = model_width // replicas
    gate_all, up_all, down_all = gather_turned((w_gate[0], w_up[0], w_down[0]), "dp", (0, 0, 1))
    gate_up_w = jnp.concatenate([gate_all, up_all], axis=1)
    received, grad_received, hidden, grad_gate_up, returned, grad_returned = full_width_pass(
        outgoing, grad_outgoing, gate_up_w, down_all, shape_out
    )
    slot_cols, grad_cols = sent_together((received, grad_received), "dp", 3, 0, 1)
    hidden_all, grad_gate_up_all = in_one_piece((hidden, grad_gate_up), "dp", 0, 1)
    slot_cols = slot_cols.reshape(replicas * own_rows, part_width)
    grad_cols = grad_cols.reshape(replicas * own_rows, part_width)
    gate_up_grad = contract_first(slot_cols, grad_gate_up_all)
    down_grad = contract_first(hidden_all, grad_cols)
    picked = (
        jnp.take(returned, slot_index, axis=0)
        .reshape(tok_count, route_count, model_width)
        .astype(jnp.float32)
    )
    mixed = jnp.sum(route_weight[:, :, None] * picked, axis=1).astype(jnp.bfloat16)
    grad_picked = (
        jnp.take(grad_returned, slot_index, axis=0)
        .reshape(tok_count, route_count, model_width)
        .astype(jnp.float32)
    )
    grad_tokens = jnp.sum(grad_picked, axis=1).astype(jnp.bfloat16)
    grad_w_gate = gate_up_grad[:, :hidden_width].astype(jnp.bfloat16)[None]
    grad_w_up = gate_up_grad[:, hidden_width:].astype(jnp.bfloat16)[None]
    grad_w_down = down_grad.astype(jnp.bfloat16)[None]
    return (mixed, grad_tokens, grad_w_gate, grad_w_up, grad_w_down)


def solution(mesh):
    finer = Mesh(
        mesh.devices.reshape(mesh.shape["dp"], 8, 4, 2), ("dp", "expert_0", "expert_1", "expert_2")
    )
    placed = (
        P(DP_EXPERT, None),
        P(DP_EXPERT, None),
        P(DP_EXPERT, None),
        P(DP_EXPERT, None),
        P(EXPERT, "dp", None),
        P(EXPERT, "dp", None),
        P(EXPERT, None, "dp"),
    )
    return jax.shard_map(
        body,
        mesh=finer,
        in_specs=placed,
        out_specs=(
            P(DP_EXPERT, None),
            P(DP_EXPERT, None),
            P(EXPERT, "dp", None),
            P(EXPERT, "dp", None),
            P(EXPERT, None, "dp"),
        ),
        check_vma=False,
    )
```

profile of v0, /device:TPU:1, one launch (start us, length us, event | category | flops | bytes accessed | tf_op | source)
XLA Modules:
  0.0 254.6 jit_solution(7288200320655958101)
XLA Ops:
  7.2 1.5 copy.61
  8.7 1.4 copy.60
  10.2 1.6 pad_maximum_fusion
  13.0 2.0 gather_fusion.2
  15.0 2.0 gather_fusion
  17.3 1.7 fusion.17
  19.6 1.9 copy.57
  21.4 11.9 %all-to-all-start = ((bf16[32,2,1,1,3,2048]{5,1,4,3,2,0:T(2,128)(2,1)}), bf16[32,2,1,1,3,2048]{5,1,4,3,2,0:T(2,128)(2,1)S(1)}, u32[]{:S(2)}, u32[]{:S(2)}) async-start(bf16[32,2,1,1,3,2048]{5,1,4,3,2,0:T(2,128)(2,1)} %copy.57), calls=%async_computation | async-start | bytes 1572864 | tf_op jit(solution)/shard_map/all_to_all | solution.py:27
  33.8 1.9 copy.65
  35.7 18.7 %all-to-all-done = bf16[32,2,1,1,3,2048]{5,1,4,3,2,0:T(2,128)(2,1)S(1)} async-done(((bf16[32,2,1,1,3,2048]{5,1,4,3,2,0:T(2,128)(2,1)}), bf16[32,2,1,1,3,2048]{5,1,4,3,2,0:T(2,128)(2,1)S(1)}, u32[]{:S(2)}, u32[]{:S(2)}) %all-to-all-start) | async-done | bytes 786464 | tf_op jit(solution)/shard_map/all_to_all | solution.py:27
  54.6 6.8 %all_to_all.58 = bf16[32,2,1,1,3,2048]{5,0,4,3,2,1:T(8,128)(2,1)S(1)} all-to-all(bf16[32,2,1,1,3,2048]{5,0,4,3,2,1:T(8,128)(2,1)S(1)} %copy.58), channel_id=1, replica_groups=mesh['dp'=4,'expert_0'=8,'expert_1'=4,'expert_2'=2] {'expert_2'}, dimensions={1} | all-to-all | bytes 1572864 | tf_op jit(solution)/shard_map/all_to_all | solution.py:27
  61.4 4.8 %all-to-all-start.4 = ((bf16[32,2,1,1,3,2048]{5,1,4,3,2,0:T(2,128)(2,1)}), bf16[32,2,1,1,3,2048]{5,1,4,3,2,0:T(2,128)(2,1)S(1)}, u32[]{:S(2)}, u32[]{:S(2)}) async-start(bf16[32,2,1,1,3,2048]{5,1,4,3,2,0:T(2,128)(2,1)} %copy.65), calls=%async_computation.4 | async-start | bytes 1572864 | tf_op jit(solution)/shard_map/all_to_all | solution.py:27
  67.0 1.4 reshape_reshape_transpose_reshape.12
  68.4 19.1 %all-to-all-done.4 = bf16[32,2,1,1,3,2048]{5,1,4,3,2,0:T(2,128)(2,1)S(1)} async-done(((bf16[32,2,1,1,3,2048]{5,1,4,3,2,0:T(2,128)(2,1)}), bf16[32,2,1,1,3,2048]{5,1,4,3,2,0:T(2,128)(2,1)S(1)}, u32[]{:S(2)}, u32[]{:S(2)}) %all-to-all-start.4) | async-done | bytes 786464 | tf_op jit(solution)/shard_map/all_to_all | solution.py:27
  87.8 6.8 %all_to_all.59 = bf16[32,2,1,1,3,2048]{5,0,4,3,2,1:T(8,128)(2,1)S(1)} all-to-all(bf16[32,2,1,1,3,2048]{5,0,4,3,2,1:T(8,128)(2,1)S(1)} %copy.66), channel_id=1, replica_groups=mesh['dp'=4,'expert_0'=8,'expert_1'=4,'expert_2'=2] {'expert_2'}, dimensions={1} | all-to-all | bytes 1572864 | tf_op jit(solution)/shard_map/all_to_all | solution.py:27
  95.3 1.4 reshape_reshape_transpose_reshape.14
  96.7 13.3 %all-gather.3.cloned.1.call-done = bf16[2048,2304]{0,1:T(8,128)(2,1)} async-done(((bf16[512,2304]{0,1:T(8,128)(2,1)}), bf16[2048,2304]{0,1:T(8,128)(2,1)}) %all-gather.3.cloned.1.call-update) | async-done | bytes 9437200 | tf_op jit(solution)/shard_map/all_gather | solution.py:41
  110.0 5.3 %fusion.2 = f32[192,1536]{1,0:T(8,128)S(1)} fusion(bf16[192,2048]{1,0:T(8,128)(2,1)} %reshape_reshape_transpose_reshape.12, bf16[2048,2304]{0,1:T(8,128)(2,1)} %all-gather.3.cloned.1.call-done), kind=kOutput, calls=%fused_computation.6 | convolution fusion | flops 1207959552 | bytes 8257536 | tf_op jit(solution)/shard_map/dot_general | solution.py:104
  115.3 3.3 %multiply_convert_fusion.3 = (bf16[192,768]{1,0:T(8,128)(2,1)S(1)}, bf16[192,768]{1,0:T(8,128)(2,1)S(1)}, bf16[192,768]{1,0:T(8,128)(2,1)S(1)}) fusion(f32[192,1536]{1,0:T(8,128)S(1)} %fusion.2, bf16[192,2048]{1,0:T(8,128)(2,1)S(1)} %copy-done.6, bf16[2048,2304]{0,1:T(8,128)(2,1)} %all-gather.3.cloned.1.call-done), kind=kOutput, calls=%fused_computation.32 | convolution fusion | flops 606339072 | bytes 5996544 | tf_op jit(solution)/shard_map/dot_general | solution.py:80
  120.3 3.6 %fusion.8 = bf16[192,2048]{1,0:T(8,128)(2,1)} fusion(bf16[192,768]{1,0:T(8,128)(2,1)S(1)} %get-tuple-element.15, bf16[2048,2304]{0,1:T(8,128)(2,1)} %all-gather.3.cloned.1.call-done), kind=kOutput, calls=%fused_computation.13 | convolution fusion | flops 604372992 | bytes 4227072 | tf_op jit(solution)/shard_map/dot_general | solution.py:108
  123.8 2.4 reshape_transpose_reshape_reshape.13
  126.3 1.9 copy.62
  128.2 9.5 %all-to-all-start.2 = ((bf16[32,2,1,1,3,2048]{5,1,4,3,2,0:T(2,128)(2,1)}), bf16[32,2,1,1,3,2048]{5,1,4,3,2,0:T(2,128)(2,1)S(1)}, u32[]{:S(2)}, u32[]{:S(2)}) async-start(bf16[32,2,1,1,3,2048]{5,1,4,3,2,0:T(2,128)(2,1)} %copy.62), calls=%async_computation.2 | async-start | bytes 1572864 | tf_op jit(solution)/shard_map/all_to_all | solution.py:27
  137.7 1.7 copy.72
  139.4 3.0 %reshape_transpose_reshape.7 = bf16[1,64,3,2048]{3,1,2,0:T(8,128)(2,1)} reshape(bf16[32,2,1,1,3,2048]{5,1,0,4,3,2:T(2,128)(2,1)} %copy.72) | data formatting | bytes 1572864 | tf_op jit(solution)/shard_map/reshape;transpose;reshape | solution.py:20
  143.2 1.2 reshape_transpose_reshape.6
  144.3 1.5 pad_maximum_fusion.1
  145.8 2.6 %copy.73 = bf16[1,128,3,2048]{1,2,0,3:T(4,128)(2,1)} copy(bf16[1,128,3,2048]{3,1,2,0:T(8,128)(2,1)S(1)} %pad_maximum_fusion.1) | data formatting | bytes 3145728 | tf_op jit(solution)/shard_map/concatenate | solution.py:56
  148.4 10.4 %all-to-all-done.2 = bf16[32,2,1,1,3,2048]{5,1,4,3,2,0:T(2,128)(2,1)S(1)} async-done(((bf16[32,2,1,1,3,2048]{5,1,4,3,2,0:T(2,128)(2,1)}), bf16[32,2,1,1,3,2048]{5,1,4,3,2,0:T(2,128)(2,1)S(1)}, u32[]{:S(2)}, u32[]{:S(2)}) %all-to-all-start.2) | async-done | bytes 786464 | tf_op jit(solution)/shard_map/all_to_all | solution.py:27
  158.7 3.8 %all-to-all-start.8 = ((bf16[1,128,3,2048]{1,2,0,3:T(4,128)(2,1)}), bf16[1,128,3,2048]{1,2,0,3:T(4,128)(2,1)S(1)}, u32[]{:S(2)}, u32[]{:S(2)}) async-start(bf16[1,128,3,2048]{1,2,0,3:T(4,128)(2,1)} %copy.73), calls=%async_computation.8 | async-start | bytes 4194304 | tf_op jit(solution)/shard_map/all_to_all | solution.py:59
  162.6 5.2 %fusion.11 = bf16[192,2048]{1,0:T(8,128)(2,1)} fusion(bf16[2048,2304]{0,1:T(8,128)(2,1)} %all-gather.3.cloned.1.call-done, bf16[192,768]{1,0:T(8,128)(2,1)} %copy-done.7, bf16[192,768]{1,0:T(8,128)(2,1)S(1)} %get-tuple-element.9), kind=kOutput, calls=%fused_computation.14 | convolution fusion | flops 1209532416 | bytes 7667712 | tf_op jit(solution)/shard_map/dot_general | solution.py:80
  167.8 3.3 %reshape_transpose_reshape_reshape.15 = bf16[32,2,1,1,3,2048]{5,4,1,0,3,2:T(4,128)(2,1)} reshape(bf16[192,2048]{1,0:T(8,128)(2,1)} %fusion.11) | data formatting | bytes 1572864 | tf_op jit(solution)/shard_map/reshape;transpose;reshape;reshape | solution.py:25
  171.0 3.1 %copy.68 = bf16[32,2,1,1,3,2048]{5,1,4,3,2,0:T(2,128)(2,1)} copy(bf16[32,2,1,1,3,2048]{5,4,1,0,3,2:T(4,128)(2,1)} %reshape_transpose_reshape_reshape.15) | data formatting | bytes 1572864 | tf_op jit(solution)/shard_map/reshape;transpose;reshape;reshape | solution.py:25
  175.3 10.9 %all-to-all-done.8 = bf16[1,128,3,2048]{1,2,0,3:T(4,128)(2,1)S(1)} async-done(((bf16[1,128,3,2048]{1,2,0,3:T(4,128)(2,1)}), bf16[1,128,3,2048]{1,2,0,3:T(4,128)(2,1)S(1)}, u32[]{:S(2)}, u32[]{:S(2)}) %all-to-all-start.8) | async-done | bytes 1572896 | tf_op jit(solution)/shard_map/all_to_all | solution.py:59
  186.1 9.8 %all_to_all.60 = bf16[32,2,1,1,3,2048]{5,0,4,3,2,1:T(8,128)(2,1)} all-to-all(bf16[32,2,1,1,3,2048]{5,0,4,3,2,1:T(8,128)(2,1)} %copy.63), channel_id=1, replica_groups=mesh['dp'=4,'expert_0'=8,'expert_1'=4,'expert_2'=2] {'expert_2'}, dimensions={1} | all-to-all | bytes 1572864 | tf_op jit(solution)/shard_map/all_to_all | solution.py:27
  196.0 9.6 %all-to-all-start.6 = ((bf16[32,2,1,1,3,2048]{5,1,4,3,2,0:T(2,128)(2,1)}), bf16[32,2,1,1,3,2048]{5,1,4,3,2,0:T(2,128)(2,1)}, u32[]{:S(2)}, u32[]{:S(2)}) async-start(bf16[32,2,1,1,3,2048]{5,1,4,3,2,0:T(2,128)(2,1)} %copy.68), calls=%async_computation.6 | async-start | bytes 1572864 | tf_op jit(solution)/shard_map/all_to_all | solution.py:27
  205.9 1.8 fusion.24
  207.7 2.8 %copy.75 = bf16[4,64,3,512]{3,2,1,0:T(4,128)(2,1)S(1)} copy(bf16[4,64,3,512]{1,3,0,2:T(8,128)(2,1)} %get-tuple-element.12) | data formatting | bytes 1572864 | tf_op jit(solution)/shard_map/split | solution.py:58
  210.5 1.4 reshape.53
  212.0 1.2 copy.76
  213.1 1.4 reshape.54
  214.6 1.8 copy.64
  217.1 9.8 %all-to-all-done.6 = bf16[32,2,1,1,3,2048]{5,1,4,3,2,0:T(2,128)(2,1)} async-done(((bf16[32,2,1,1,3,2048]{5,1,4,3,2,0:T(2,128)(2,1)}), bf16[32,2,1,1,3,2048]{5,1,4,3,2,0:T(2,128)(2,1)}, u32[]{:S(2)}, u32[]{:S(2)}) %all-to-all-start.6) | async-done | bytes 786464 | tf_op jit(solution)/shard_map/all_to_all | solution.py:27
  226.9 1.4 copy.69
  228.3 6.7 %all_to_all.61 = bf16[32,2,1,1,3,2048]{5,0,4,3,2,1:T(8,128)(2,1)S(1)} all-to-all(bf16[32,2,1,1,3,2048]{5,0,4,3,2,1:T(8,128)(2,1)S(1)} %copy.69), channel_id=1, replica_groups=mesh['dp'=4,'expert_0'=8,'expert_1'=4,'expert_2'=2] {'expert_2'}, dimensions={1} | all-to-all | bytes 1572864 | tf_op jit(solution)/shard_map/all_to_all | solution.py:27
  240.3 3.1 %convolution_convert_fusion = bf16[512,1536]{1,0:T(8,128)(2,1)S(1)} fusion(bf16[768,512]{1,0:T(8,128)(2,1)S(1)} %copy-done.5, bf16[768,2304]{1,0:T(8,128)(2,1)} %all-gather.5.cloned.1.call-done), kind=kOutput, calls=%fused_computation.8 | convolution fusion | flops 1208745984 | bytes 4718592 | tf_op jit(solution)/shard_map/dot_general | solution.py:86
  243.4 1.2 slice_bitcast_fusion
  244.8 3.0 %fusion.15 = bf16[1,768,512]{2,1,0:T(8,128)(2,1)} fusion(bf16[768,512]{1,0:T(8,128)(2,1)S(1)} %copy-done.4, bf16[768,2304]{1,0:T(8,128)(2,1)} %all-gather.5.cloned.1.call-done), kind=kOutput, calls=%fused_computation.20 | convolution fusion | flops 604372992 | bytes 2752512 | tf_op jit(solution)/shard_map/dot_general | solution.py:86
  (55 shorter events, 14.4 us)
Async XLA Ops:
  7.2 5.8 %copy-start = (bf16[128,2048]{1,0:T(8,128)(2,1)S(1)}, bf16[128,2048]{1,0:T(8,128)(2,1)}, u32[]{:S(2)}) copy-start(bf16[128,2048]{1,0:T(8,128)(2,1)} %param.12) | copy-start | bytes 1572868
  7.2 3.0 %copy-start.3 = (bf16[1,768,512]{2,1,0:T(8,128)(2,1)S(1)}, bf16[1,768,512]{2,1,0:T(8,128)(2,1)}, u32[]{:S(2)}) copy-start(bf16[1,768,512]{2,1,0:T(8,128)(2,1)} %param.17) | copy-start | bytes 2359300
  7.2 102.8 %all-gather.3.cloned.1.call-start = ((), (), s32[]{:S(2)}) async-start(), calls=%async_computation.9 | async-start | bytes 11796480 | tf_op jit(solution)/shard_map/all_gather | solution.py:41
  11.7 0.7 copy-start.8
  13.0 2.0 copy-start.2
  15.0 2.1 copy-start.9
  21.4 32.9 %all-to-all-start = ((bf16[32,2,1,1,3,2048]{5,1,4,3,2,0:T(2,128)(2,1)}), bf16[32,2,1,1,3,2048]{5,1,4,3,2,0:T(2,128)(2,1)S(1)}, u32[]{:S(2)}, u32[]{:S(2)}) async-start(bf16[32,2,1,1,3,2048]{5,1,4,3,2,0:T(2,128)(2,1)} %copy.57), calls=%async_computation | async-start | bytes 1572864 | tf_op jit(solution)/shard_map/all_to_all | solution.py:27
  61.4 26.2 %all-to-all-start.4 = ((bf16[32,2,1,1,3,2048]{5,1,4,3,2,0:T(2,128)(2,1)}), bf16[32,2,1,1,3,2048]{5,1,4,3,2,0:T(2,128)(2,1)S(1)}, u32[]{:S(2)}, u32[]{:S(2)}) async-start(bf16[32,2,1,1,3,2048]{5,1,4,3,2,0:T(2,128)(2,1)} %copy.65), calls=%async_computation.4 | async-start | bytes 1572864 | tf_op jit(solution)/shard_map/all_to_all | solution.py:27
  66.2 174.1 %all-gather.5.cloned.1.call-start = ((), (), s32[]{:S(2)}) async-start(), calls=%async_computation.10 | async-start | bytes 4423680 | tf_op jit(solution)/shard_map/all_gather | solution.py:68
  96.7 18.6 %copy-start.6 = (bf16[192,2048]{1,0:T(8,128)(2,1)S(1)}, bf16[192,2048]{1,0:T(8,128)(2,1)}, u32[]{:S(2)}) copy-start(bf16[192,2048]{1,0:T(8,128)(2,1)} %reshape_reshape_transpose_reshape.14) | copy-start | bytes 2359300
  118.5 0.7 copy-start.7
  128.2 30.6 %all-to-all-start.2 = ((bf16[32,2,1,1,3,2048]{5,1,4,3,2,0:T(2,128)(2,1)}), bf16[32,2,1,1,3,2048]{5,1,4,3,2,0:T(2,128)(2,1)S(1)}, u32[]{:S(2)}, u32[]{:S(2)}) async-start(bf16[32,2,1,1,3,2048]{5,1,4,3,2,0:T(2,128)(2,1)} %copy.62), calls=%async_computation.2 | async-start | bytes 1572864 | tf_op jit(solution)/shard_map/all_to_all | solution.py:27
  158.7 27.4 %all-to-all-start.8 = ((bf16[1,128,3,2048]{1,2,0,3:T(4,128)(2,1)}), bf16[1,128,3,2048]{1,2,0,3:T(4,128)(2,1)S(1)}, u32[]{:S(2)}, u32[]{:S(2)}) async-start(bf16[1,128,3,2048]{1,2,0,3:T(4,128)(2,1)} %copy.73), calls=%async_computation.8 | async-start | bytes 4194304 | tf_op jit(solution)/shard_map/all_to_all | solution.py:59
  196.0 30.9 %all-to-all-start.6 = ((bf16[32,2,1,1,3,2048]{5,1,4,3,2,0:T(2,128)(2,1)}), bf16[32,2,1,1,3,2048]{5,1,4,3,2,0:T(2,128)(2,1)}, u32[]{:S(2)}, u32[]{:S(2)}) async-start(bf16[32,2,1,1,3,2048]{5,1,4,3,2,0:T(2,128)(2,1)} %copy.68), calls=%async_computation.6 | async-start | bytes 1572864 | tf_op jit(solution)/shard_map/all_to_all | solution.py:27
  237.4 3.0 %copy-start.5 = (bf16[768,512]{1,0:T(8,128)(2,1)S(1)}, bf16[768,512]{1,0:T(8,128)(2,1)}, u32[]{:S(2)}) copy-start(bf16[768,512]{1,0:T(8,128)(2,1)} %reshape.53) | copy-start | bytes 2359300
  243.4 1.4 copy-start.4
  243.4 4.3 %copy-start.1 = (bf16[128,2048]{1,0:T(8,128)(2,1)S(1)}, bf16[128,2048]{1,0:T(8,128)(2,1)}, u32[]{:S(2)}) copy-start(bf16[128,2048]{1,0:T(8,128)(2,1)} %param.12) | copy-start | bytes 1572868
Sparse Core Ops, SparseCore 0:
  11.9 98.0 all-gather.2
  120.4 46.3 all-gather.4
where the time goes:
time: 256 us; the launch traced here: 255 us
  waiting for transfers between devices  82.2 us (32%)
  local copies, waits for them, and re-layouts  56.2 us (22%)
  starting transfers between devices  39.8 us (16%)
  blocking collectives  30.1 us (12%)
  matrix products  23.3 us (9%)
  between operations  14.4 us (6%)
  other arithmetic  8.59 us (3%)
    all_to_all x4, waiting for transfers between devices, turned_blocks(): lax.all_to_all(tiles, axes[k], split_axis=k, concat_axis=k, tiled=True)  58 us
    all_to_all x4, starting transfers between devices, turned_blocks(): lax.all_to_all(tiles, axes[k], split_axis=k, concat_axis=k, tiled=True)  35.9 us
    all_to_all x4, blocking collectives, turned_blocks(): lax.all_to_all(tiles, axes[k], split_axis=k, concat_axis=k, tiled=True)  30.1 us
    another operation x8, local copies, waits for them, and re-layouts, turned_blocks(): tiles = tiles.reshape(*lengths, *tiles.shape[1:])  15.4 us
    all_gather x1, waiting for transfers between devices, gather_turned(): filled = lax.all_gather(both, axis, axis=0, tiled=True)  13.3 us
    all_to_all x1, waiting for transfers between devices, sent_together(): lax.all_to_all(both, axis, split_axis=split_dim, concat_axis=concat_dim,...  10.9 us
    all_to_all x10, local copies, waits for them, and re-layouts, turned_blocks(): lax.all_to_all(tiles, axes[k], split_axis=k, concat_axis=k, tiled=True)  9.33 us
    dot_general x2, matrix products, contract_last(): lax.dot_general(left_side, right_side, (((1,), (1,)), ((), ())), preferre...  8.43 us
  transfers between devices with their start and end apart: 7, of which 6 were waited for; matrix products, arithmetic and copies ran while one was open for 26% of the time, Pallas kernels for 0%

commit v1 on v0

--- a/solution.py
+++ b/solution.py
@@ -38,7 +38,9 @@
     turned = [jnp.moveaxis(a, dim, 0) for a, dim in zip(arrays, dims)]
     widths = [t[0].size for t in turned]
     both = jnp.concatenate([t.reshape(-1, w) for t, w in zip(turned, widths)], axis=1)
-    filled = lax.all_gather(both, axis, axis=0, tiled=True)
+    filled = jnp.concatenate(
+        lax.all_to_all(jnp.stack([both] * lax.axis_size(axis)), axis, 0, 0), axis=0
+    )
     tiles = jnp.split(filled, [sum(widths[:k]) for k in range(1, len(widths))], axis=1)
     return tuple(
         (

time: 256 us -> 347 us (1.36)
  waiting for transfers between devices: 82.2 us -> 163 us
  starting transfers between devices: 39.8 us -> 50.2 us
  blocking collectives: 30.1 us -> 22.4 us
  local copies, waits for them, and re-layouts: 56.2 us -> 62 us
    all_to_all x0 -> x1, waiting for transfers between devices: none -> 99.9 us  [gather_turned(): lax.all_to_all(jnp.stack([both] * lax.axis_size(axis)), axis, 0, 0)]
    all_gather x1 -> x0, waiting for transfers between devices: 13.3 us -> none  [gather_turned(): filled = lax.all_gather(both, axis, axis=0, tiled=True)]
    all_to_all x4 -> x3, blocking collectives: 30.1 us -> 22.4 us  [turned_blocks(): lax.all_to_all(tiles, axes[k], split_axis=k, concat_axis=k, tiled=True)]
    all_to_all x4 -> x5, waiting for transfers between devices: 58 us -> 51.1 us  [turned_blocks(): lax.all_to_all(tiles, axes[k], split_axis=k, concat_axis=k, tiled=True)]
    all_to_all x0 -> x1, starting transfers between devices: none -> 5.82 us  [gather_turned(): lax.all_to_all(jnp.stack([both] * lax.axis_size(axis)), axis, 0, 0)]
    all_to_all x10, local copies, waits for them, and re-layouts: 9.33 us -> 14.8 us  [turned_blocks(): lax.all_to_all(tiles, axes[k], split_axis=k, concat_axis=k, tiled=True)]
    all_to_all x4 -> x5, starting transfers between devices: 35.9 us -> 40.4 us  [turned_blocks(): lax.all_to_all(tiles, axes[k], split_axis=k, concat_axis=k, tiled=True)]
    another operation x0 -> x1, local copies, waits for them, and re-layouts: none -> 4.26 us  [gather_turned(): jnp.stack([both] * lax.axis_size(axis))]
  transfers between devices with their start and end apart: 7 -> 8, of which waited for: 6 -> 6; matrix products, arithmetic and copies ran while one was open for 26% -> 19% of each run, Pallas kernels for 0% -> 0%
where the time goes in v1:
time: 347 us; the launch traced here: 345 us
  waiting for transfers between devices  163 us (47%)
  local copies, waits for them, and re-layouts  62 us (18%)
  starting transfers between devices  50.2 us (14%)
  blocking collectives  22.4 us (6%)
  matrix products  22.3 us (6%)
  between operations  14.4 us (4%)
  other arithmetic  10.8 us (3%)
    all_to_all x1, waiting for transfers between devices, gather_turned(): lax.all_to_all(jnp.stack([both] * lax.axis_size(axis)), axis, 0, 0)  99.9 us
    all_to_all x5, waiting for transfers between devices, turned_blocks(): lax.all_to_all(tiles, axes[k], split_axis=k, concat_axis=k, tiled=True)  51.1 us
    all_to_all x5, starting transfers between devices, turned_blocks(): lax.all_to_all(tiles, axes[k], split_axis=k, concat_axis=k, tiled=True)  40.4 us
    all_to_all x3, blocking collectives, turned_blocks(): lax.all_to_all(tiles, axes[k], split_axis=k, concat_axis=k, tiled=True)  22.4 us
    all_to_all x10, local copies, waits for them, and re-layouts, turned_blocks(): lax.all_to_all(tiles, axes[k], split_axis=k, concat_axis=k, tiled=True)  14.8 us
    another operation x8, local copies, waits for them, and re-layouts, turned_blocks(): tiles = tiles.reshape(*lengths, *tiles.shape[1:])  13.5 us
    all_to_all x1, waiting for transfers between devices, sent_together(): lax.all_to_all(both, axis, split_axis=split_dim, concat_axis=concat_dim,...  11.9 us
    dot_general x2, matrix products, contract_last(): lax.dot_general(left_side, right_side, (((1,), (1,)), ((), ())), preferre...  7.89 us
  transfers between devices with their start and end apart: 8, of which 6 were waited for; matrix products, arithmetic and copies ran while one was open for 19% of the time, Pallas kernels for 0%

profile of v1, /device:TPU:1, one launch (start us, length us, event | category | flops | bytes accessed | tf_op | source)
XLA Modules:
  0.0 345.1 jit_solution(15088311088940179623)
XLA Ops:
  9.9 2.0 gather_fusion
  12.0 2.0 gather_fusion.2
  14.1 1.7 fusion.17
  16.4 1.9 copy.61
  18.2 11.9 %all-to-all-start = ((bf16[32,2,1,1,3,2048]{5,1,4,3,2,0:T(2,128)(2,1)}), bf16[32,2,1,1,3,2048]{5,1,4,3,2,0:T(2,128)(2,1)S(1)}, u32[]{:S(2)}, u32[]{:S(2)}) async-start(bf16[32,2,1,1,3,2048]{5,1,4,3,2,0:T(2,128)(2,1)} %copy.61), calls=%async_computation | async-start | bytes 1572864 | tf_op jit(solution)/shard_map/all_to_all | solution.py:27
  30.6 1.9 copy.70
  32.5 18.7 %all-to-all-done = bf16[32,2,1,1,3,2048]{5,1,4,3,2,0:T(2,128)(2,1)S(1)} async-done(((bf16[32,2,1,1,3,2048]{5,1,4,3,2,0:T(2,128)(2,1)}), bf16[32,2,1,1,3,2048]{5,1,4,3,2,0:T(2,128)(2,1)S(1)}, u32[]{:S(2)}, u32[]{:S(2)}) %all-to-all-start) | async-done | bytes 786464 | tf_op jit(solution)/shard_map/all_to_all | solution.py:27
  51.2 5.9 %all-to-all-start.5 = ((bf16[32,2,1,1,3,2048]{5,1,4,3,2,0:T(2,128)(2,1)}), bf16[32,2,1,1,3,2048]{5,1,4,3,2,0:T(2,128)(2,1)}, u32[]{:S(2)}, u32[]{:S(2)}) async-start(bf16[32,2,1,1,3,2048]{5,1,4,3,2,0:T(2,128)(2,1)} %copy.70), calls=%async_computation.5 | async-start | bytes 1572864 | tf_op jit(solution)/shard_map/all_to_all | solution.py:27
  59.4 1.8 pad_maximum_fusion
  61.2 2.5 copy.66
  63.7 2.3 copy.62
  66.0 10.9 %all-to-all-done.5 = bf16[32,2,1,1,3,2048]{5,1,4,3,2,0:T(2,128)(2,1)} async-done(((bf16[32,2,1,1,3,2048]{5,1,4,3,2,0:T(2,128)(2,1)}), bf16[32,2,1,1,3,2048]{5,1,4,3,2,0:T(2,128)(2,1)}, u32[]{:S(2)}, u32[]{:S(2)}) %all-to-all-start.5) | async-done | bytes 786464 | tf_op jit(solution)/shard_map/all_to_all | solution.py:27
  76.9 8.5 %all-to-all-start.1 = ((bf16[32,2,1,1,3,2048]{5,0,4,3,2,1:T(8,128)(2,1)}), bf16[32,2,1,1,3,2048]{5,0,4,3,2,1:T(8,128)(2,1)}, u32[]{:S(2)}, u32[]{:S(2)}) async-start(bf16[32,2,1,1,3,2048]{5,0,4,3,2,1:T(8,128)(2,1)} %copy.62), calls=%async_computation.1 | async-start | bytes 1572864 | tf_op jit(solution)/shard_map/all_to_all | solution.py:27
  85.3 2.3 copy.71
  87.6 6.0 %all_to_all.63 = bf16[32,2,1,1,3,2048]{5,0,4,3,2,1:T(8,128)(2,1)} all-to-all(bf16[32,2,1,1,3,2048]{5,0,4,3,2,1:T(8,128)(2,1)} %copy.71), channel_id=1, replica_groups=mesh['dp'=4,'expert_0'=8,'expert_1'=4,'expert_2'=2] {'expert_2'}, dimensions={1} | all-to-all | bytes 1572864 | tf_op jit(solution)/shard_map/all_to_all | solution.py:27
  93.6 4.3 %stack.2 = bf16[4,512,2304]{2,1,0:T(8,128)(2,1)} broadcast(bf16[512,2304]{1,0:T(8,128)(2,1)S(1)} %copy-done.3), dimensions={1,2} | broadcast | bytes 11796480 | tf_op jit(solution)/shard_map/stack | solution.py:42
  97.8 5.8 %all-to-all-start.2 = ((bf16[4,512,2304]{2,1,0:T(8,128)(2,1)}), bf16[4,512,2304]{2,1,0:T(8,128)(2,1)}, u32[]{:S(2)}, u32[]{:S(2)}) async-start(bf16[4,512,2304]{2,1,0:T(8,128)(2,1)} %stack.2), calls=%async_computation.2 | async-start | bytes 18874368 | tf_op jit(solution)/shard_map/all_to_all | solution.py:42
  103.9 1.8 copy.63
  105.7 1.4 reshape_reshape_transpose_reshape.12
  108.5 99.9 %all-to-all-done.2 = bf16[4,512,2304]{2,1,0:T(8,128)(2,1)} async-done(((bf16[4,512,2304]{2,1,0:T(8,128)(2,1)}), bf16[4,512,2304]{2,1,0:T(8,128)(2,1)}, u32[]{:S(2)}, u32[]{:S(2)}) %all-to-all-start.2) | async-done | bytes 9437216 | tf_op jit(solution)/shard_map/all_to_all | solution.py:42
  208.4 4.5 %fusion.2 = f32[192,1536]{1,0:T(8,128)S(1)} fusion(bf16[192,2048]{1,0:T(8,128)(2,1)} %reshape_reshape_transpose_reshape.12, bf16[2048,2304]{1,0:T(8,128)(2,1)} %bitcast.6), kind=kOutput, calls=%fused_computation.6 | convolution fusion | flops 1207959552 | bytes 8257536 | tf_op jit(solution)/shard_map/dot_general | solution.py:106
  212.9 2.8 multiply_convert_fusion.3
  216.7 5.1 %fusion.11 = bf16[192,2048]{1,0:T(8,128)(2,1)S(1)} fusion(bf16[2048,2304]{1,0:T(8,128)(2,1)} %bitcast.6, bf16[192,768]{1,0:T(8,128)(2,1)S(1)} %get-tuple-element.10, bf16[192,768]{1,0:T(8,128)(2,1)S(1)} %get-tuple-element.9), kind=kOutput, calls=%fused_computation.14 | convolution fusion | flops 1209532416 | bytes 7667712 | tf_op jit(solution)/shard_map/dot_general | solution.py:82
  222.3 1.9 copy.73
  224.2 4.8 %all-to-all-start.7 = ((bf16[32,2,1,1,3,2048]{5,1,4,3,2,0:T(2,128)(2,1)}), bf16[32,2,1,1,3,2048]{5,1,4,3,2,0:T(2,128)(2,1)S(1)}, u32[]{:S(2)}, u32[]{:S(2)}) async-start(bf16[32,2,1,1,3,2048]{5,1,4,3,2,0:T(2,128)(2,1)} %copy.73), calls=%async_computation.7 | async-start | bytes 1572864 | tf_op jit(solution)/shard_map/all_to_all | solution.py:27
  229.0 1.9 copy.76
  234.1 1.5 pad_maximum_fusion.1
  235.6 2.6 copy.78
  238.2 11.7 %all-to-all-done.7 = bf16[32,2,1,1,3,2048]{5,1,4,3,2,0:T(2,128)(2,1)S(1)} async-done(((bf16[32,2,1,1,3,2048]{5,1,4,3,2,0:T(2,128)(2,1)}), bf16[32,2,1,1,3,2048]{5,1,4,3,2,0:T(2,128)(2,1)S(1)}, u32[]{:S(2)}, u32[]{:S(2)}) %all-to-all-start.7) | async-done | bytes 786464 | tf_op jit(solution)/shard_map/all_to_all | solution.py:27
  249.9 3.8 %all-to-all-start.9 = ((bf16[1,128,3,2048]{1,2,0,3:T(4,128)(2,1)}), bf16[1,128,3,2048]{1,2,0,3:T(4,128)(2,1)S(1)}, u32[]{:S(2)}, u32[]{:S(2)}) async-start(bf16[1,128,3,2048]{1,2,0,3:T(4,128)(2,1)} %copy.78), calls=%async_computation.9 | async-start | bytes 4194304 | tf_op jit(solution)/shard_map/all_to_all | solution.py:61
  253.7 3.9 %fusion.8 = bf16[192,2048]{1,0:T(8,128)(2,1)} fusion(bf16[192,768]{1,0:T(8,128)(2,1)S(1)} %get-tuple-element.15, bf16[2048,2304]{1,0:T(8,128)(2,1)} %bitcast.6), kind=kOutput, calls=%fused_computation.13 | convolution fusion | flops 604372992 | bytes 4227072 | tf_op jit(solution)/shard_map/dot_general | solution.py:110
  257.7 3.3 reshape_transpose_reshape_reshape.13
  260.9 3.1 copy.67
  265.2 11.9 %all-to-all-done.9 = bf16[1,128,3,2048]{1,2,0,3:T(4,128)(2,1)S(1)} async-done(((bf16[1,128,3,2048]{1,2,0,3:T(4,128)(2,1)}), bf16[1,128,3,2048]{1,2,0,3:T(4,128)(2,1)S(1)}, u32[]{:S(2)}, u32[]{:S(2)}) %all-to-all-start.9) | async-done | bytes 1572896 | tf_op jit(solution)/shard_map/all_to_all | solution.py:61
  277.1 9.7 %all_to_all.64 = bf16[32,2,1,1,3,2048]{5,0,4,3,2,1:T(8,128)(2,1)} all-to-all(bf16[32,2,1,1,3,2048]{5,0,4,3,2,1:T(8,128)(2,1)} %copy.74), channel_id=1, replica_groups=mesh['dp'=4,'expert_0'=8,'expert_1'=4,'expert_2'=2] {'expert_2'}, dimensions={1} | all-to-all | bytes 1572864 | tf_op jit(solution)/shard_map/all_to_all | solution.py:27
  286.8 9.4 %all-to-all-start.3 = ((bf16[32,2,1,1,3,2048]{5,1,4,3,2,0:T(2,128)(2,1)}), bf16[32,2,1,1,3,2048]{5,1,4,3,2,0:T(2,128)(2,1)}, u32[]{:S(2)}, u32[]{:S(2)}) async-start(bf16[32,2,1,1,3,2048]{5,1,4,3,2,0:T(2,128)(2,1)} %copy.67), calls=%async_computation.3 | async-start | bytes 1572864 | tf_op jit(solution)/shard_map/all_to_all | solution.py:27
  296.4 1.8 fusion.24
  298.2 2.8 copy.81
  301.1 1.4 reshape.60
  302.5 1.2 copy.80
  303.7 1.4 reshape.59
  305.1 1.8 copy.75
  307.6 9.8 %all-to-all-done.3 = bf16[32,2,1,1,3,2048]{5,1,4,3,2,0:T(2,128)(2,1)} async-done(((bf16[32,2,1,1,3,2048]{5,1,4,3,2,0:T(2,128)(2,1)}), bf16[32,2,1,1,3,2048]{5,1,4,3,2,0:T(2,128)(2,1)}, u32[]{:S(2)}, u32[]{:S(2)}) %all-to-all-start.3) | async-done | bytes 786464 | tf_op jit(solution)/shard_map/all_to_all | solution.py:27
  317.4 1.4 copy.68
  318.8 6.7 %all_to_all.65 = bf16[32,2,1,1,3,2048]{5,0,4,3,2,1:T(8,128)(2,1)S(1)} all-to-all(bf16[32,2,1,1,3,2048]{5,0,4,3,2,1:T(8,128)(2,1)S(1)} %copy.68), channel_id=1, replica_groups=mesh['dp'=4,'expert_0'=8,'expert_1'=4,'expert_2'=2] {'expert_2'}, dimensions={1} | all-to-all | bytes 1572864 | tf_op jit(solution)/shard_map/all_to_all | solution.py:27
  330.9 3.1 convolution_convert_fusion
  334.0 1.2 slice_bitcast_fusion
  335.3 3.0 fusion.15
  (59 shorter events, 19.9 us)
Async XLA Ops:
  7.2 2.8 copy-start
  9.9 2.0 copy-start.2
  12.0 2.0 copy-start.10
  18.2 32.9 %all-to-all-start = ((bf16[32,2,1,1,3,2048]{5,1,4,3,2,0:T(2,128)(2,1)}), bf16[32,2,1,1,3,2048]{5,1,4,3,2,0:T(2,128)(2,1)S(1)}, u32[]{:S(2)}, u32[]{:S(2)}) async-start(bf16[32,2,1,1,3,2048]{5,1,4,3,2,0:T(2,128)(2,1)} %copy.61), calls=%async_computation | async-start | bytes 1572864 | tf_op jit(solution)/shard_map/all_to_all | solution.py:27
  30.6 26.5 %copy-start.8 = (bf16[1,512,768]{2,1,0:T(8,128)(2,1)S(1)}, bf16[1,512,768]{2,1,0:T(8,128)(2,1)}, u32[]{:S(2)}) copy-start(bf16[1,512,768]{2,1,0:T(8,128)(2,1)} %param.15) | copy-start | bytes 2359300
  32.5 25.8 %copy-start.9 = (bf16[1,512,768]{2,1,0:T(8,128)(2,1)S(1)}, bf16[1,512,768]{2,1,0:T(8,128)(2,1)}, u32[]{:S(2)}) copy-start(bf16[1,512,768]{2,1,0:T(8,128)(2,1)} %param.16) | copy-start | bytes 2359300
  51.2 8.2 %copy-start.5 = (bf16[32,2,1,1,3,2048]{5,1,4,3,2,0:T(2,128)(2,1)}, bf16[32,2,1,1,3,2048]{5,1,4,3,2,0:T(2,128)(2,1)S(1)}, u32[]{:S(2)}) copy-start(bf16[32,2,1,1,3,2048]{5,1,4,3,2,0:T(2,128)(2,1)S(1)} %all-to-all-done) | copy-start | bytes 2359300
  51.2 25.7 %all-to-all-start.5 = ((bf16[32,2,1,1,3,2048]{5,1,4,3,2,0:T(2,128)(2,1)}), bf16[32,2,1,1,3,2048]{5,1,4,3,2,0:T(2,128)(2,1)}, u32[]{:S(2)}, u32[]{:S(2)}) async-start(bf16[32,2,1,1,3,2048]{5,1,4,3,2,0:T(2,128)(2,1)} %copy.70), calls=%async_computation.5 | async-start | bytes 1572864 | tf_op jit(solution)/shard_map/all_to_all | solution.py:27
  66.0 27.6 %copy-start.3 = (bf16[512,2304]{1,0:T(8,128)(2,1)S(1)}, bf16[512,2304]{1,0:T(8,128)(2,1)}, u32[]{:S(2)}) copy-start(bf16[512,2304]{1,0:T(8,128)(2,1)} %copy.66) | copy-start | bytes 7077892
  76.9 10.7 %all-to-all-start.1 = ((bf16[32,2,1,1,3,2048]{5,0,4,3,2,1:T(8,128)(2,1)}), bf16[32,2,1,1,3,2048]{5,0,4,3,2,1:T(8,128)(2,1)}, u32[]{:S(2)}, u32[]{:S(2)}) async-start(bf16[32,2,1,1,3,2048]{5,0,4,3,2,1:T(8,128)(2,1)} %copy.62), calls=%async_computation.1 | async-start | bytes 1572864 | tf_op jit(solution)/shard_map/all_to_all | solution.py:27
  97.8 110.6 %all-to-all-start.2 = ((bf16[4,512,2304]{2,1,0:T(8,128)(2,1)}), bf16[4,512,2304]{2,1,0:T(8,128)(2,1)}, u32[]{:S(2)}, u32[]{:S(2)}) async-start(bf16[4,512,2304]{2,1,0:T(8,128)(2,1)} %stack.2), calls=%async_computation.2 | async-start | bytes 18874368 | tf_op jit(solution)/shard_map/all_to_all | solution.py:42
  103.7 3.5 %copy-start.4 = (bf16[32,2,1,1,3,2048]{5,0,4,3,2,1:T(8,128)(2,1)S(1)}, bf16[32,2,1,1,3,2048]{5,0,4,3,2,1:T(8,128)(2,1)}, u32[]{:S(2)}) copy-start(bf16[32,2,1,1,3,2048]{5,0,4,3,2,1:T(8,128)(2,1)} %all_to_all.63) | copy-start | bytes 2359300
  103.7 227.2 %all-gather.2.cloned.1.call-start = ((), (), s32[]{:S(2)}) async-start(), calls=%async_computation.10 | async-start | bytes 4423680 | tf_op jit(solution)/shard_map/all_gather | solution.py:70
  224.2 25.7 %all-to-all-start.7 = ((bf16[32,2,1,1,3,2048]{5,1,4,3,2,0:T(2,128)(2,1)}), bf16[32,2,1,1,3,2048]{5,1,4,3,2,0:T(2,128)(2,1)S(1)}, u32[]{:S(2)}, u32[]{:S(2)}) async-start(bf16[32,2,1,1,3,2048]{5,1,4,3,2,0:T(2,128)(2,1)} %copy.73), calls=%async_computation.7 | async-start | bytes 1572864 | tf_op jit(solution)/shard_map/all_to_all | solution.py:27
  249.9 27.2 %all-to-all-start.9 = ((bf16[1,128,3,2048]{1,2,0,3:T(4,128)(2,1)}), bf16[1,128,3,2048]{1,2,0,3:T(4,128)(2,1)S(1)}, u32[]{:S(2)}, u32[]{:S(2)}) async-start(bf16[1,128,3,2048]{1,2,0,3:T(4,128)(2,1)} %copy.78), calls=%async_computation.9 | async-start | bytes 4194304 | tf_op jit(solution)/shard_map/all_to_all | solution.py:61
  286.8 30.7 %all-to-all-start.3 = ((bf16[32,2,1,1,3,2048]{5,1,4,3,2,0:T(2,128)(2,1)}), bf16[32,2,1,1,3,2048]{5,1,4,3,2,0:T(2,128)(2,1)}, u32[]{:S(2)}, u32[]{:S(2)}) async-start(bf16[32,2,1,1,3,2048]{5,1,4,3,2,0:T(2,128)(2,1)} %copy.67), calls=%async_computation.3 | async-start | bytes 1572864 | tf_op jit(solution)/shard_map/all_to_all | solution.py:27
  327.9 3.0 copy-start.7
  333.9 1.4 copy-start.6
  334.0 4.3 %copy-start.1 = (bf16[128,2048]{1,0:T(8,128)(2,1)S(1)}, bf16[128,2048]{1,0:T(8,128)(2,1)}, u32[]{:S(2)}) copy-start(bf16[128,2048]{1,0:T(8,128)(2,1)} %param.11) | copy-start | bytes 1572868
Sparse Core Ops, SparseCore 0:
  216.9 40.3 all-gather.1
